TPU v7x, 256 devices: a whole 4x4x8 slice. The times are simulated.
256 devices in a mesh: grp: 32 (over z_hi, x, core), fsdp: 8 (over z_lo, y).
Axes of the slice: x: 4, y: 4, z: 8 (z_hi: 4, z_lo: 2; z = z_hi * 2 + z_lo), core: 2. Of those that a mesh axis runs over, the one named last changes fastest.
Arguments:
- tokens: bfloat16 [98304, 3584], P(('grp', 'fsdp')), may hold values from -6 to 6
- target: bfloat16 [98304, 1024], P(('grp', 'fsdp')), may hold values from -6 to 6
- weight: bfloat16 [3584, 1024], P('fsdp'), may hold values from -0.09375 to 0.09375
- factor_a: bfloat16 [3584, 512], P('fsdp'), may hold values from -6 to 6
- factor_b: bfloat16 [512, 1024], replicated, may hold values from -6 to 6
- counts: int32 [512], replicated, may hold values from 1 to 768, 98304 in all
- cand_index: int32 [512, 2], replicated, may hold values from 0 to 511
Outputs:
- update: float32 [3584, 1024], P('fsdp')
- scores: float32 [512], replicated
Inputs may be any that keep to these rules, and one draw needn't show every extreme that they name: The counts sum to 98304; candidate i owns the tokens from counts[0] + ... + counts[i-1] on.
All inputs are finite; a program needn't handle non-finite values.
Results may differ from a plain program's by a relative error of at most 0.003.
Values may be sent and summed in bfloat16 or wider, within the bound.
A program may use at most 64 MiB of HBM per device.

v0:
```python
import jax
import jax.numpy as jnp
from jax import lax
from jax.sharding import Mesh
from jax.sharding import PartitionSpec as P

D = 3584
FSDP = ("fsdp_0", "fsdp_1")
GRP_FSDP = ("grp_0", "grp_1", "grp_2", "fsdp_0", "fsdp_1")


def side_by_side(arrays, axis, dim, along):
    ends, at = ([], 0)
    for a in arrays[:-1]:
        at += a.shape[along]
        ends.append(at)
    both = jnp.concatenate(arrays, axis=along)
    return tuple(jnp.split(lax.all_gather(both, axis, axis=dim, tiled=True), ends, axis=along))


def one_axis_at_a_time(value, axes):
    for axis in axes:
        value = lax.psum(value, axis)
    return value


def per_device(tokens, target, weight, factor_a, factor_b, counts, cand_index):
    rows = tokens.shape[0]
    pool_size = factor_a.shape[1]
    total_cands = counts.shape[0]
    noise = 0.5 * D ** (-0.5)
    pieces = side_by_side((weight, factor_a), FSDP, 0, 1)
    columns = tokens
    base = jnp.dot(columns, pieces[0], preferred_element_type=jnp.float32)
    pool_scores = jnp.dot(columns, pieces[1], preferred_element_type=jnp.float32)
    ends = jnp.cumsum(counts)
    position = lax.axis_index(GRP_FSDP) * rows + jnp.arange(rows, dtype=jnp.int32)
    owner = jnp.sum((ends[None, :] <= position[:, None]).astype(jnp.int32), axis=1)
    left_index = cand_index[:, 0]
    right_index = cand_index[:, 1]
    tok_a = jnp.take(left_index, owner)
    tok_b = jnp.take(right_index, owner)
    pool_ids = jnp.arange(pool_size, dtype=jnp.int32)
    picked = jnp.sum(jnp.where(tok_a[:, None] == pool_ids[None, :], pool_scores, 0.0), axis=1)
    right_rows = jnp.take(factor_b, tok_b, axis=0).astype(jnp.float32)
    output = base + noise * picked[:, None] * right_rows
    diff = output - target.astype(jnp.float32)
    loss = jnp.mean(diff * diff, axis=1)
    cand_ids = jnp.arange(total_cands, dtype=jnp.int32)
    partial_value = jnp.sum(
        jnp.where(owner[:, None] == cand_ids[None, :], loss[:, None], 0.0), axis=0
    )
    totals = one_axis_at_a_time(partial_value, GRP_FSDP)
    fitness = -totals / counts.astype(jnp.float32)
    middle = jnp.mean(fitness)
    variance = jnp.mean((fitness - middle) ** 2)
    scores = (fitness - middle) / jnp.sqrt(variance + 1e-06)
    selector = (pool_ids[:, None] == left_index[None, :]).astype(jnp.bfloat16)
    columns = jnp.dot(factor_a, selector, preferred_element_type=jnp.float32)
    scaled = (columns * scores[None, :]).astype(jnp.bfloat16)
    chosen_rows = jnp.take(factor_b, right_index, axis=0)
    summed_update = jnp.dot(scaled, chosen_rows, preferred_element_type=jnp.float32)
    update = summed_update / jnp.sqrt(jnp.float32(total_cands))
    return (update, scores)


def solution(mesh):
    split = Mesh(
        mesh.devices.reshape(4, 4, 2, 2, 4), ("grp_0", "grp_1", "grp_2", "fsdp_0", "fsdp_1")
    )
    placed = (P(GRP_FSDP, None), P(GRP_FSDP, None), P(FSDP, None), P(FSDP, None), P(), P(), P())
    return jax.shard_map(
        per_device, mesh=split, in_specs=placed, out_specs=(P(FSDP, None), P()), check_vma=False
    )
```

profile of v0, /device:TPU:2, one launch (start us, length us, event | category | flops | bytes accessed | tf_op | source)
XLA Modules:
  0.0 193.4 jit_solution(16207273097916178139)
XLA Ops:
  7.2 0.0 copy-start
  7.2 0.0 copy-start.4
  7.2 0.0 all-gather.2.cloned.1.call-start
  7.2 2.6 %pad_maximum_fusion = bf16[448,1536]{1,0:T(8,128)(2,1)} fusion(bf16[448,512]{1,0:T(8,128)(2,1)} %param.12, bf16[448,1024]{1,0:T(8,128)(2,1)} %param.11), kind=kLoop, calls=%fused_computation.13 | loop fusion | flops 2752512 | bytes 2752512 | tf_op jit(solution)/shard_map/concatenate | solution.py:17
  9.9 0.0 all-gather.2.cloned.1.call-update
  9.9 0.3 reduce-window.9
  10.2 0.1 slice.14
  10.4 0.1 slice_reduce_fusion
  10.5 0.1 add_bitcast_fusion
  10.5 0.2 convert_reduce_fusion
  10.8 3.9 %gather_fusion.2 = s32[384]{0:T(512)} fusion(s32[512]{0:T(512)S(1)} %bitcast.23, s32[1024]{0:T(1024)S(1)} %pad_clamp_fusion.2), kind=kCustom, calls=%fused_computation.clone | custom fusion | bytes 4608 | tf_op jit(solution)/shard_map/jit(_take)/gather | solution.py:41
  14.8 2.8 %gather_fusion.3 = s32[384]{0:T(512)S(1)} fusion(s32[512]{0:T(512)S(1)} %bitcast.25, s32[1024]{0:T(1024)S(1)} %pad_clamp_fusion.2), kind=kCustom, calls=%fused_computation.1.clone | custom fusion | bytes 4608 | tf_op jit(solution)/shard_map/jit(_take)/gather | solution.py:42
  17.6 0.5 compare_and_fusion.1
  18.1 4.1 %gather_fusion = bf16[384,1024]{1,0:T(8,128)(2,1)S(1)} fusion(bf16[512,1024]{1,0:T(8,128)(2,1)} %param.13, s32[1024]{0:T(1024)S(1)} %pad_clamp_fusion.1), kind=kCustom, calls=%fused_computation.2 | custom fusion | bytes 1574400 | tf_op jit(solution)/shard_map/jit(_take)/gather | solution.py:45
  22.2 1.2 copy.13
  23.5 2.3 %copy.14 = bf16[384,1024]{0,1:T(8,128)(2,1)} copy(bf16[384,1024]{1,0:T(8,128)(2,1)} %param.10) | data formatting | bytes 1572864 | tf_op args[1]
  25.8 0.0 copy-start.6
  25.8 4.8 %gather_fusion.1 = bf16[512,1024]{1,0:T(8,128)(2,1)} fusion(bf16[512,1024]{1,0:T(8,128)(2,1)} %param.13, s32[1024]{0:T(1024)S(1)} %pad_clamp_fusion), kind=kCustom, calls=%fused_computation.3 | custom fusion | bytes 2099200 | tf_op jit(solution)/shard_map/jit(_take)/gather | solution.py:61
  30.7 101.8 %all-gather.2.cloned.1.call-done = bf16[3584,1536]{1,0:T(8,128)(2,1)} async-done(((bf16[448,1536]{1,0:T(8,128)(2,1)}), bf16[3584,1536]{1,0:T(8,128)(2,1)}) %all-gather.2.cloned.1.call-update) | async-done | bytes 11010064 | tf_op jit(solution)/shard_map/all_gather | solution.py:18
  132.4 4.2 %fusion.16 = f32[384]{0:T(512)S(1)} fusion(bf16[384,3584]{1,0:T(8,128)(2,1)S(1)} %copy-done, bf16[3584,1536]{1,0:T(8,128)(2,1)} %all-gather.2.cloned.1.call-done, s32[384]{0:T(512)S(1)} %broadcast_select_fusion), kind=kOutput, calls=%fused_computation.18 | convolution fusion | flops 1409875584 | bytes 6425600 | tf_op jit(solution)/shard_map/dot_general | solution.py:35
  136.7 0.0 copy-start.5
  136.7 7.3 %fusion.6 = f32[384]{0:T(512)S(1)} fusion(bf16[384,1024]{0,1:T(8,128)(2,1)S(1)} %copy-done.2, bf16[384,3584]{1,0:T(8,128)(2,1)S(1)} %copy-done, bf16[3584,1536]{1,0:T(8,128)(2,1)} %all-gather.2.cloned.1.call-done, bf16[384,1024]{0,1:T(8,128)(2,1)S(1)} %copy-done.1, f32[384]{0:T(512)S(1)} %broadcast_multiply_fusion.1, pred[384]{0:T(512)(128)(4,1)S(1)} %copy-done.8), kind=kOutput, calls=%fused_computation.11 | convolution fusion | flops 2821717504 | bytes 11668864 | tf_op jit(solution)/shard_map/dot_general | solution.py:34
  144.0 0.2 select_reduce_fusion
  144.2 11.9 %psum.35 = f32[512]{0:T(512)S(1)} all-reduce(f32[512]{0:T(512)S(1)} %select_reduce_fusion), channel_id=1, replica_groups=mesh['grp_0'=4,'grp_1'=4,'grp_2'=2,'fsdp_0'=2,'fsdp_1'=4] {'grp_0'}, use_global_device_ids=true, to_apply=%region_6.8 | all-reduce | flops 512 | bytes 4096 | tf_op jit(solution)/shard_map/psum | solution.py:23
  156.0 8.6 %psum.36 = f32[512]{0:T(512)S(1)} all-reduce(f32[512]{0:T(512)S(1)} %psum.35), channel_id=1, replica_groups=mesh['grp_0'=4,'grp_1'=4,'grp_2'=2,'fsdp_0'=2,'fsdp_1'=4] {'grp_1'}, use_global_device_ids=true, to_apply=%region_7.9 | all-reduce | flops 512 | bytes 4096 | tf_op jit(solution)/shard_map/psum | solution.py:23
  164.6 2.5 %psum.37 = f32[512]{0:T(512)S(1)} all-reduce(f32[512]{0:T(512)S(1)} %psum.36), channel_id=1, replica_groups=mesh['grp_0'=4,'grp_1'=4,'grp_2'=2,'fsdp_0'=2,'fsdp_1'=4] {'grp_2'}, use_global_device_ids=true, to_apply=%region_8.10 | all-reduce | flops 512 | bytes 4096 | tf_op jit(solution)/shard_map/psum | solution.py:23
  167.0 4.9 %psum.38 = f32[512]{0:T(512)S(1)} all-reduce(f32[512]{0:T(512)S(1)} %psum.37), channel_id=1, replica_groups=mesh['grp_0'=4,'grp_1'=4,'grp_2'=2,'fsdp_0'=2,'fsdp_1'=4] {'fsdp_0'}, use_global_device_ids=true, to_apply=%region_9.11 | all-reduce | flops 512 | bytes 4096 | tf_op jit(solution)/shard_map/psum | solution.py:23
  172.0 8.4 %psum.39 = f32[512]{0:T(512)S(1)} all-reduce(f32[512]{0:T(512)S(1)} %psum.38), channel_id=1, replica_groups=mesh['grp_0'=4,'grp_1'=4,'grp_2'=2,'fsdp_0'=2,'fsdp_1'=4] {'fsdp_1'}, use_global_device_ids=true, to_apply=%region_10.12 | all-reduce | flops 512 | bytes 4096 | tf_op jit(solution)/shard_map/psum | solution.py:23
  180.4 0.6 fusion.26
  181.7 0.6 multiply_reduce_fusion
  183.0 0.0 copy-start.7
  183.0 3.5 %convolution_multiply_fusion = f32[448,1024]{1,0:T(8,128)} fusion(bf16[448,512]{1,0:T(8,128)(2,1)} %param.12, bf16[512,1024]{1,0:T(8,128)(2,1)} %gather_fusion.1, pred[512]{0:T(512)(128)(4,1)S(1)} %get-tuple-element.7, s32[512]{0:T(512)S(1)} %bitcast.24, f32[512]{0:T(512)S(1)} %subtract_divide_fusion), kind=kOutput, calls=%fused_computation.12 | convolution fusion | flops 706347008 | bytes 3346944 | tf_op jit(solution)/shard_map/dot_general | solution.py:62
  (25 shorter events, 0.1 us)
Async XLA Ops:
  7.2 125.3 %copy-start = (bf16[384,3584]{1,0:T(8,128)(2,1)S(1)}, bf16[384,3584]{1,0:T(8,128)(2,1)}, u32[]{:S(2)}) copy-start(bf16[384,3584]{1,0:T(8,128)(2,1)} %param.9) | copy-start | bytes 8257540
  7.2 2.7 %copy-start.4 = (s32[512]{0:T(512)S(1)}, s32[512]{0:T(512)}, u32[]{:S(2)}) copy-start(s32[512]{0:T(512)} %param.14) | copy-start | bytes 6148
  7.2 3.6 %copy-start.3 = (s32[512,2]{0,1:T(2,128)S(1)}, s32[512,2]{0,1:T(2,128)}, u32[]{:S(2)}) copy-start(s32[512,2]{0,1:T(2,128)} %param.15) | copy-start | bytes 12292
  7.2 125.2 %all-gather.2.cloned.1.call-start = ((), (), s32[]{:S(2)}) async-start(), calls=%async_computation | async-start | bytes 12386304 | tf_op jit(solution)/shard_map/all_gather | solution.py:18
  25.8 4.8 %copy-start.6 = (s32[384]{0:T(512)S(1)}, s32[384]{0:T(512)}, u32[]{:S(2)}) copy-start(s32[384]{0:T(512)} %gather_fusion.2) | copy-start | bytes 4612
  30.6 106.0 %copy-start.1 = (bf16[384,1024]{0,1:T(8,128)(2,1)S(1)}, bf16[384,1024]{0,1:T(8,128)(2,1)}, u32[]{:S(2)}) copy-start(bf16[384,1024]{0,1:T(8,128)(2,1)} %copy.13) | copy-start | bytes 2359300
  132.4 4.2 %copy-start.2 = (bf16[384,1024]{0,1:T(8,128)(2,1)S(1)}, bf16[384,1024]{0,1:T(8,128)(2,1)}, u32[]{:S(2)}) copy-start(bf16[384,1024]{0,1:T(8,128)(2,1)} %copy.14) | copy-start | bytes 2359300
  132.4 4.3 %copy-start.8 = (pred[384]{0:T(512)(128)(4,1)S(1)}, pred[384]{0:T(512)(128)(4,1)}, u32[]{:S(2)}) copy-start(pred[384]{0:T(512)(128)(4,1)} %get-tuple-element.5) | copy-start | bytes 1156
  136.7 43.7 %copy-start.5 = (s32[512]{0:T(512)S(1)}, s32[512]{0:T(512)}, u32[]{:S(2)}) copy-start(s32[512]{0:T(512)} %param.14) | copy-start | bytes 6148
  183.0 3.6 %copy-start.7 = (f32[512]{0:T(512)}, f32[512]{0:T(512)S(1)}, u32[]{:S(2)}) copy-start(f32[512]{0:T(512)S(1)} %subtract_divide_fusion) | copy-start | bytes 6148
Sparse Core Ops, SparseCore 0:
  10.4 122.0 all-gather.1
where the time goes:
time: 195 us; the launch traced here: 193 us
  waiting for transfers between devices  102 us (52%)
  blocking collectives  36.2 us (19%)
  local copies, waits for them, and re-layouts  19.5 us (10%)
  between operations  15.6 us (8%)
  matrix products  15 us (8%)
  other arithmetic  5.26 us (3%)
    all_gather x1, waiting for transfers between devices, side_by_side(): lax.all_gather(both, axis, axis=dim, tiled=True)  102 us
    psum x5, blocking collectives, one_axis_at_a_time(): value = lax.psum(value, axis)  36.2 us
    dot_general x1, matrix products, per_device(): base = jnp.dot(columns, pieces[0], preferred_element_type=jnp.float32)  7.28 us
    gather x2, local copies, waits for them, and re-layouts, per_device(): right_rows = jnp.take(factor_b, tok_b, axis=0).astype(jnp.float32)  5.35 us
    gather x1, local copies, waits for them, and re-layouts, per_device(): chosen_rows = jnp.take(factor_b, right_index, axis=0)  4.83 us
    dot_general x1, matrix products, per_device(): jnp.dot(columns, pieces[1], preferred_element_type=jnp.float32)  4.22 us
    gather x1, local copies, waits for them, and re-layouts, per_device(): tok_a = jnp.take(left_index, owner)  3.94 us
  transfers between devices with their start and end apart: 1, of which 1 were waited for; matrix products, arithmetic and copies ran while one was open for 11% of the time, Pallas kernels for 0%

commit v1 on v0

v1 whole, which is shorter than its diff:
```python
import functools

import jax
import jax.numpy as jnp
from jax import lax
from jax.experimental import pallas as pl
from jax.experimental.pallas import tpu as pltpu
from jax.sharding import Mesh
from jax.sharding import PartitionSpec as P

D = 3584
F32 = jnp.float32
BF16 = jnp.bfloat16
MESH = pl.DeviceIdType.MESH
FSDP = ("fsdp_0", "fsdp_1")
GRP_FSDP = ("grp_0", "grp_1", "grp_2", "fsdp_0", "fsdp_1")

INBOUND = {
    "y+": ((0, 1, "m1"), (0, 1, "m2"), (0, 2, "m1"), (0, 1, "c2"), (0, 1, "c1"), (0, 2, "m2"), (0, 2, "c1"), (1, 2, "t2")),
    "y-": ((0, 3, "m1"), (0, 3, "m2"), (0, 3, "c1"), (0, 3, "c2"), (1, 3, "m2"), (0, 2, "c2"), (1, 2, "m2"), (1, 2, "c1")),
    "z+": ((1, 0, "m1"), (1, 0, "t1"), (1, 3, "m1"), (1, 1, "m1"), (1, 1, "t1"), (1, 3, "c1"), (1, 1, "c2"), (1, 2, "c2")),
    "z-": ((1, 0, "m2"), (1, 0, "c1"), (1, 0, "c2"), (1, 1, "m2"), (1, 2, "m1"), (1, 3, "c2"), (1, 1, "c1")),
    "x+": ((0, 1, "t1"), (1, 0, "t2"), (1, 3, "t1"), (0, 3, "t2"), (1, 3, "t2"), (0, 2, "t2")),
    "x-": ((0, 3, "t1"), (0, 1, "t2"), (0, 2, "t1"), (1, 1, "t2"), (1, 2, "t1")),
}
LINK_STEP = {"y+": (0, 1, 0), "y-": (0, -1, 0), "z+": (0, 0, 1), "z-": (0, 0, -1), "x+": (1, 0, 0), "x-": (-1, 0, 0)}
SWAP = {"m1": "t1", "m2": "t2", "t1": "m1", "t2": "m2"}
ROLES = ("m1", "m2", "t1", "t2", "c1", "c2")
GROUPS = {"a": ("m1", "t1"), "p": ("m2", "t2"), "q": ("c1", "c2")}
PIECE_US, HOP_US, LEAD_US, TOKENS_US = 2.48, 1.7, 2.5, 5.0


def source(link, o, d, role):
    if link == "y+":
        return (o, (d - 1) % 4, role)
    if link == "y-":
        return (o, (d + 1) % 4, role)
    if link[0] == "z":
        return (1 - o, d, role)
    return (o, d, SWAP[role])


def timeline():
    arrival = {(0, 0, role): 0.0 for role in ROLES}
    free = dict.fromkeys(INBOUND, 0.0)
    waiting = {link: list(items) for link, items in INBOUND.items()}
    events = []
    while any(waiting.values()):
        ready = [
            (max(free[link], arrival[source(link, *items[0])]), link)
            for link, items in waiting.items()
            if items and source(link, *items[0]) in arrival
        ]
        start, link = min(ready)
        item = waiting[link].pop(0)
        free[link] = start + PIECE_US
        arrival[item] = start + PIECE_US + HOP_US
        issue = max(arrival[source(link, *item)], start - LEAD_US)
        events.append((issue, 0, ("send", link, item)))
    for o in range(2):
        for d in range(4):
            for group, roles in GROUPS.items():
                when = max(TOKENS_US, *(arrival[(o, d, role)] for role in roles))
                events.append((when, 1, ("product", (o, d), group)))
    return events


def one_hot(row, first, size):
    lines = lax.broadcasted_iota(jnp.int32, (size, row.shape[1]), 0) + first
    return (lines == row).astype(F32).astype(BF16)


def across(a, b):
    return lax.dot_general(a, b, (((1,), (1,)), ((), ())), preferred_element_type=F32)


def kernel(
    tokens, target, weight, factor_a, factor_b, counts, index, totals, asel_out, bsel_out,
    tok, tgt, buf, fb, fa, cnt, idx, acc_a, acc_w, owns, picks, brow, s_part, s_recv, asel, bsel,
    ar_x, ar_y, ar_z, local, send_sem, recv_sem, tok_send, tok_recv, s_send, s_got, ar_send, ar_recv,
):
    zh, x, c, zl, y = (lax.axis_index(n) for n in GRP_FSDP)
    z = zh * 2 + zl
    par = lax.rem(x, 2)
    rows, depth, cands = tokens.shape[0], weight.shape[0], counts.shape[1]
    noise = 0.5 * D ** (-0.5)

    def at(dx=0, dy=0, dz=0, dc=0):
        there = lax.rem(z + dz + 8, 8)
        return (there // 2, lax.rem(x + dx + 4, 4), lax.rem(c + dc + 2, 2), lax.rem(there, 2), lax.rem(y + dy + 4, 4))

    def piece_of(role):
        return {"m1": par, "m2": 2 + par, "t1": 1 - par, "t2": 3 - par, "c1": 4, "c2": 5}[role]

    def rows_of(d):
        return pl.ds(pl.multiple_of(lax.rem(y + d, 2) * 64, 64), depth)

    def columns(start, size):
        return pl.ds(pl.multiple_of(start, 128), size)

    copies = {}

    def bring(name, src, dst):
        copies[name] = pltpu.make_async_copy(src, dst, local.at[len(copies)])
        copies[name].start()

    for role in ROLES:
        j = piece_of(role)
        if role in ("m1", "t1"):
            src = factor_a.at[:, columns(c * 256 + j * 128, 128)]
        else:
            src = weight.at[:, columns(c * 512 + (j - 2) * 128, 128)]
        bring(role, src, buf.at[0, j, rows_of(0)])
    bring("cnt", counts, cnt)
    bring("idx", index, idx)
    bring("tok", tokens, tok.at[0])
    bring("tgt", target.at[:, columns(c * 512, 512)], tgt.at[0])
    bring("fb", factor_b, fb)
    bring("fa", factor_a, fa)

    zero = jnp.zeros((64, 128), BF16)
    for d in range(4):
        gap = pl.multiple_of((1 - lax.rem(y + d, 2)) * depth, 64)
        for o in range(2):
            for j in range(6):
                buf[o * 4 + d, j, pl.ds(gap, 64), :] = zero

    ar_peers = [
        [dict(dx=dx, dc=dc) for dx in range(4) for dc in range(2) if dx or dc],
        [dict(dy=dy) for dy in range(1, 4)],
        [dict(dz=dz) for dz in range(1, 8)],
    ]
    barrier = pltpu.get_barrier_semaphore()
    for group in ar_peers:
        for peer in group:
            pl.semaphore_signal(barrier, inc=1, device_id=at(**peer), device_id_type=MESH)
    pl.semaphore_wait(barrier, sum(map(len, ar_peers)))

    items = [item for link in INBOUND for item in INBOUND[link]]
    sends, waited = [], set()

    def need(item):
        if item in waited:
            return
        waited.add(item)
        o, d, role = item
        if (o, d) == (0, 0):
            copies[role].wait()
            return
        k = items.index(item)
        place = buf.at[o * 4 + d, piece_of(role), rows_of(d)]
        pltpu.make_async_remote_copy(
            src_ref=place, dst_ref=place, send_sem=send_sem.at[k], recv_sem=recv_sem.at[k],
            device_id=at(dc=1), device_id_type=MESH,
        ).wait_recv()

    def send(link, item):
        so, sd, srole = source(link, *item)
        need((so, sd, srole))
        k = items.index(item)
        dx, dy, dz = LINK_STEP[link]
        j = piece_of(srole)
        copy = pltpu.make_async_remote_copy(
            src_ref=buf.at[so * 4 + sd, j, rows_of(sd)],
            dst_ref=buf.at[item[0] * 4 + item[1], j, rows_of(sd)],
            send_sem=send_sem.at[k], recv_sem=recv_sem.at[k],
            device_id=at(-dx, -dy, -dz), device_id_type=MESH,
        )
        copy.start()
        sends.append(copy)

    swaps = [
        pltpu.make_async_remote_copy(
            src_ref=src, dst_ref=dst, send_sem=tok_send.at[k], recv_sem=tok_recv.at[k],
            device_id=at(dc=1), device_id_type=MESH,
        )
        for k, (src, dst) in enumerate(
            ((tokens, tok.at[1]), (target.at[:, columns((1 - c) * 512, 512)], tgt.at[1]))
        )
    ]

    def start_swaps():
        for copy in swaps:
            copy.start()

    def owners():
        copies["cnt"].wait()
        copies["idx"].wait()
        count = cnt[...]
        upto = (
            lax.broadcasted_iota(jnp.int32, (cands, cands), 0) <= lax.broadcasted_iota(jnp.int32, (cands, cands), 1)
        ).astype(F32).astype(BF16)
        high = jnp.broadcast_to((count >> 7).astype(F32), (16, cands)).astype(BF16)
        low = jnp.broadcast_to((count & 127).astype(F32), (16, cands)).astype(BF16)
        ends = jnp.dot(high, upto, preferred_element_type=F32) * 128.0 + jnp.dot(
            low, upto, preferred_element_type=F32
        )
        ends = ends[0:1, :].astype(jnp.int32)
        starts = ends - count
        for i in range(2):
            who = lax.rem(c + i, 2)
            block = ((zh * 4 + x) * 2 + who) * 8 + zl * 4 + y
            token = lax.broadcasted_iota(jnp.int32, (rows, cands), 0) + block * rows
            owns[i] = ((starts <= token) & (token < ends)).astype(F32).astype(BF16)

    def left_picks():
        left = one_hot(idx[0:1, :], c * 256, 256)
        for i in range(2):
            picks[i] = across(owns[i], left)

    def right_rows():
        copies["fb"].wait()
        right = one_hot(idx[1:2, :], 0, fb.shape[0])
        mine = fb[:, columns(c * 512, 512)]
        for i in range(2):
            chosen = across(owns[i], right).astype(BF16)
            brow[i] = jnp.dot(chosen, mine, preferred_element_type=F32)

    out_copies = []

    def chosen_left():
        copies["fa"].wait()
        left = one_hot(idx[0:1, :], 0, fa.shape[1])
        asel[...] = jnp.dot(fa[...], left, preferred_element_type=F32).astype(BF16)
        copy = pltpu.make_async_copy(asel, asel_out, local.at[len(copies)])
        copy.start()
        out_copies.append(copy)

    def chosen_right():
        size = (cands, cands)
        line, lane = lax.broadcasted_iota(jnp.int32, size, 0), lax.broadcasted_iota(jnp.int32, size, 1)
        row = idx[1:2, :].astype(F32)
        column = jnp.sum(jnp.where(line == lane, row, 0.0), axis=1, keepdims=True)
        right = (column == lane.astype(F32)).astype(F32).astype(BF16)
        bsel[...] = jnp.dot(right, fb[...], preferred_element_type=F32).astype(BF16)
        copy = pltpu.make_async_copy(bsel, bsel_out, local.at[len(copies) + 1])
        copy.start()
        out_copies.append(copy)

    seen, left_over = set(), {"a": 8}
    s_copies = [
        pltpu.make_async_remote_copy(
            src_ref=s_part.at[i], dst_ref=s_recv.at[1 - i], send_sem=s_send.at[i], recv_sem=s_got.at[i],
            device_id=at(dc=1), device_id_type=MESH,
        )
        for i in range(2)
    ]

    def product(slot, group):
        o, d = slot
        for role in GROUPS[group]:
            need((o, d, role))
        first = lax.rem(zl + o, 2) * 4 + lax.rem(y + d, 4)
        window = columns(first // 2 * 896 + lax.rem(first, 2) * 384, 512)
        j = "apq".index(group) * 2
        block = jnp.concatenate([buf[o * 4 + d, j], buf[o * 4 + d, j + 1]], axis=1)
        acc, lanes = (acc_a, slice(0, 256)) if group == "a" else (acc_w, slice(j * 128 - 256, j * 128))
        for i in range(2):
            if i == 0 and "tok" not in waited:
                copies["tok"].wait()
            if i == 1 and "tok" not in waited:
                swaps[0].wait_recv()
                waited.add("tok")
            part = jnp.dot(tok[i, :, window], block, preferred_element_type=F32)
            if group in seen:
                acc[i, :, lanes] += part
            else:
                acc[i, :, lanes] = part
        seen.add(group)
        if group == "a":
            left_over["a"] -= 1
            if left_over["a"] == 0:
                for i in range(2):
                    kept = jnp.where(picks[i] > 0.5, acc_a[i], 0.0)
                    s_part[i] = kept[:, :128] + kept[:, 128:]
                    s_copies[i].start()

    def perturb():
        copies["tgt"].wait()
        swaps[1].wait_recv()
        for copy in s_copies:
            copy.wait_recv()
        for i in range(2):
            score = jnp.sum(s_part[i] + s_recv[i], axis=1, keepdims=True) * noise
            acc_w[i] += score * brow[i] - tgt[i].astype(F32)

    events = timeline()
    after_a = max(when for when, _, what in events if what[0] == "product" and what[2] == "a")
    events += [
        (0.05, 2, (start_swaps,)), (0.5, 2, (owners,)), (1.0, 2, (left_picks,)), (1.5, 2, (right_rows,)),
        (2.0, 2, (chosen_left,)), (2.5, 2, (chosen_right,)), (after_a + 1.2, 2, (perturb,)),
    ]
    for _, _, what in sorted(events, key=lambda event: event[:2]):
        if what[0] == "send":
            send(*what[1:])
        elif what[0] == "product":
            product(*what[1:])
        else:
            what[0]()

    total = jnp.zeros((1, cands), F32)
    for i in range(2):
        diff = acc_w[i]
        square = diff * diff
        square = (square[:, :128] + square[:, 128:256]) + (square[:, 256:384] + square[:, 384:])
        loss = jnp.sum(square, axis=1, keepdims=True) * (1.0 / 1024)
        total += jnp.sum(owns[i].astype(F32) * loss, axis=0, keepdims=True)
    first = 0
    for group, ring, me, number in (
        (ar_peers[0], ar_x, x * 2 + c, lambda dx=0, dc=0: lax.rem(x - dx + 4, 4) * 2 + lax.rem(c - dc + 2, 2)),
        (ar_peers[1], ar_y, y, lambda dy: lax.rem(y - dy + 4, 4)),
        (ar_peers[2], ar_z, z, lambda dz: lax.rem(z - dz + 8, 8)),
    ):
        ring[me] = total
        out = [
            pltpu.make_async_remote_copy(
                src_ref=ring.at[me], dst_ref=ring.at[me], send_sem=ar_send.at[first + k], recv_sem=ar_recv.at[first + k],
                device_id=at(**peer), device_id_type=MESH,
            )
            for k, peer in enumerate(group)
        ]
        for copy in out:
            copy.start()
        for k, peer in enumerate(group):
            place = ring.at[number(**peer)]
            pltpu.make_async_remote_copy(
                src_ref=place, dst_ref=place, send_sem=ar_send.at[first + k], recv_sem=ar_recv.at[first + k],
                device_id=at(**peer), device_id_type=MESH,
            ).wait_recv()
        total = ring[0]
        for k in range(1, ring.shape[0]):
            total += ring[k]
        sends.extend(out)
        first += len(group)
    totals[...] = total
    for copy in sends + swaps + s_copies:
        copy.wait_send()
    for copy in out_copies:
        copy.wait()


def gather_and_sum(tokens, target, weight, factor_a, factor_b, counts, index):
    rows, depth = tokens.shape[0], weight.shape[0]
    cands, pool, out = counts.shape[1], factor_a.shape[1], weight.shape[1]
    links = sum(map(len, INBOUND.values()))
    dma = pltpu.SemaphoreType.DMA
    return pl.pallas_call(
        kernel,
        name="gather_and_sum",
        out_shape=(
            jax.ShapeDtypeStruct((1, cands), F32),
            jax.ShapeDtypeStruct((depth, cands), BF16),
            jax.ShapeDtypeStruct((cands, out), BF16),
        ),
        in_specs=[pl.BlockSpec(memory_space=pl.ANY)] * 7,
        out_specs=(
            pl.BlockSpec(memory_space=pltpu.VMEM),
            pl.BlockSpec(memory_space=pl.ANY),
            pl.BlockSpec(memory_space=pl.ANY),
        ),
        scratch_shapes=[
            pltpu.VMEM((2, rows, D), BF16),
            pltpu.VMEM((2, rows, out // 2), BF16),
            pltpu.VMEM((8, 6, depth + 64, 128), BF16),
            pltpu.VMEM((pool, out), BF16),
            pltpu.VMEM((depth, pool), BF16),
            pltpu.VMEM((1, cands), jnp.int32),
            pltpu.VMEM((2, cands), jnp.int32),
            pltpu.VMEM((2, rows, pool // 2), F32),
            pltpu.VMEM((2, rows, out // 2), F32),
            pltpu.VMEM((2, rows, cands), BF16),
            pltpu.VMEM((2, rows, pool // 2), F32),
            pltpu.VMEM((2, rows, out // 2), F32),
            pltpu.VMEM((2, rows, 128), F32),
            pltpu.VMEM((2, rows, 128), F32),
            pltpu.VMEM((depth, cands), BF16),
            pltpu.VMEM((cands, out), BF16),
            pltpu.VMEM((8, 1, cands), F32),
            pltpu.VMEM((4, 1, cands), F32),
            pltpu.VMEM((8, 1, cands), F32),
            dma((14,)),
            dma((links,)),
            dma((links,)),
            dma((2,)),
            dma((2,)),
            dma((2,)),
            dma((2,)),
            dma((17,)),
            dma((17,)),
        ],
        compiler_params=pltpu.CompilerParams(collective_id=0, has_side_effects=True, vmem_limit_bytes=48 << 20),
    )(tokens, target, weight, factor_a, factor_b, counts, index)


def finish_kernel(totals, counts, asel, bsel, update, scores):
    cands = counts.shape[1]
    fitness = -totals[...] / counts[...].astype(F32)
    middle = jnp.mean(fitness, axis=1, keepdims=True)
    spread = jnp.mean((fitness - middle) ** 2, axis=1, keepdims=True)
    score = (fitness - middle) / jnp.sqrt(spread + 1e-06)
    scores[...] = score
    scaled = (asel[...].astype(F32) * score).astype(BF16)
    update[...] = jnp.dot(scaled, bsel[...], preferred_element_type=F32) * (cands**-0.5)


def finish(totals, counts, asel, bsel):
    depth, cands = asel.shape
    out = bsel.shape[1]
    block = depth // 4
    row = pl.BlockSpec((1, cands), lambda i: (0, 0))
    return pl.pallas_call(
        finish_kernel,
        name="finish",
        grid=(4,),
        out_shape=(jax.ShapeDtypeStruct((depth, out), F32), jax.ShapeDtypeStruct((1, cands), F32)),
        in_specs=[
            row,
            row,
            pl.BlockSpec((block, cands), lambda i: (i, 0)),
            pl.BlockSpec((cands, out), lambda i: (0, 0)),
        ],
        out_specs=(pl.BlockSpec((block, out), lambda i: (i, 0)), row),
    )(totals, counts, asel, bsel)


def per_device(tokens, target, weight, factor_a, factor_b, counts, cand_index):
    counts = counts.reshape(1, -1)
    totals, asel, bsel = gather_and_sum(tokens, target, weight, factor_a, factor_b, counts, cand_index.T)
    update, scores = finish(totals, counts, asel, bsel)
    return (update, scores.reshape(-1))


def solution(mesh):
    split = Mesh(mesh.devices.reshape(4, 4, 2, 2, 4), GRP_FSDP)
    placed = (P(GRP_FSDP, None), P(GRP_FSDP, None), P(FSDP, None), P(FSDP, None), P(), P(), P())
    return jax.shard_map(
        per_device, mesh=split, in_specs=placed, out_specs=(P(FSDP, None), P()), check_vma=False
    )
```

time: 195 us -> 60.7 us (0.31)
  waiting for transfers between devices: 102 us -> 0 us
  Pallas kernels: 0 us -> 51.4 us
  blocking collectives: 36.2 us -> 0 us
  matrix products: 15 us -> 0 us
  between operations: 15.6 us -> 0.66 us
  local copies, waits for them, and re-layouts: 19.5 us -> 8.24 us
  other arithmetic: 5.26 us -> 0 us
    all_gather x1 -> x0, waiting for transfers between devices: 102 us -> none  [side_by_side(): lax.all_gather(both, axis, axis=dim, tiled=True)]
    pallas_call x0 -> x2, Pallas kernels: none -> 51.4 us  [the longest x1 46.7 us: gather_and_sum(): pl.pallas_call(kernel, name='gather_and_sum', out_shape=(jax.ShapeDtypeSt...]
    psum x5 -> x0, blocking collectives: 36.2 us -> none  [one_axis_at_a_time(): value = lax.psum(value, axis)]
    gather x5 -> x0, local copies, waits for them, and re-layouts: 16.9 us -> none  [the longest x2 5.35 us: per_device(): right_rows = jnp.take(factor_b, tok_b, axis=0).astype(jnp.float32)]
    dot_general x3 -> x0, matrix products: 15 us -> none  [the longest x1 7.28 us: per_device(): base = jnp.dot(columns, pieces[0], preferred_element_type=jnp.float32)]
    unnamed x19 -> x18, local copies, waits for them, and re-layouts: 2.35 us -> 8.24 us
    concatenate x1 -> x0, other arithmetic: 2.64 us -> none  [side_by_side(): both = jnp.concatenate(arrays, axis=along)]
  transfers between devices with their start and end apart: 1 -> 0, of which waited for: 1 -> 0; matrix products, arithmetic and copies ran while one was open for 11% -> 0% of each run, Pallas kernels for 0% -> 0%
where the time goes in v1:
time: 60.7 us; the launch traced here: 60.3 us
  Pallas kernels  51.4 us (85%)
  local copies, waits for them, and re-layouts  8.24 us (14%)
  between operations  0.66 us (1%)
    pallas_call x1, Pallas kernels, gather_and_sum(): pl.pallas_call(kernel, name='gather_and_sum', out_shape=(jax.ShapeDtypeSt...  46.7 us
    unnamed x18, local copies, waits for them, and re-layouts  8.24 us
    pallas_call x1, Pallas kernels, finish(): pl.pallas_call(finish_kernel, name='finish', grid=(4,), out_shape=(jax.Sh...  4.7 us

profile of v1, /device:TPU:2, one launch (start us, length us, event | category | flops | bytes accessed | tf_op | source)
XLA Modules:
  0.0 60.3 jit_solution(8662801197058575773)
XLA Ops:
  0.6 0.0 copy-start
  0.6 1.2 %copy-done = bf16[512,1024]{1,0:T(8,128)(2,1)S(1)} copy-done((bf16[512,1024]{1,0:T(8,128)(2,1)S(1)}, bf16[512,1024]{1,0:T(8,128)(2,1)}, u32[]{:S(2)}) %copy-start) | copy-done | bytes 1048600
  1.9 0.0 copy-start.2
  1.9 1.2 %copy-done.2 = bf16[448,1024]{1,0:T(8,128)(2,1)S(1)} copy-done((bf16[448,1024]{1,0:T(8,128)(2,1)S(1)}, bf16[448,1024]{1,0:T(8,128)(2,1)}, u32[]{:S(2)}) %copy-start.2) | copy-done | bytes 917528
  3.0 0.0 copy-start.3
  3.0 1.1 %copy-done.3 = bf16[384,1024]{1,0:T(8,128)(2,1)S(1)} copy-done((bf16[384,1024]{1,0:T(8,128)(2,1)S(1)}, bf16[384,1024]{1,0:T(8,128)(2,1)}, u32[]{:S(2)}) %copy-start.3) | copy-done | bytes 786456
  4.2 0.0 copy-start.4
  4.2 1.0 %copy-done.4 = bf16[448,512]{1,0:T(8,128)(2,1)S(1)} copy-done((bf16[448,512]{1,0:T(8,128)(2,1)S(1)}, bf16[448,512]{1,0:T(8,128)(2,1)}, u32[]{:S(2)}) %copy-start.4) | copy-done | bytes 458776
  5.2 0.0 copy-start.6
  5.2 0.7 %copy-done.6 = s32[512]{0:T(512)S(1)} copy-done((s32[512]{0:T(512)S(1)}, s32[512]{0:T(512)}, u32[]{:S(2)}) %copy-start.6) | copy-done | bytes 2072
  5.9 0.0 copy-start.7
  5.9 0.7 %copy-done.7 = s32[512,2]{0,1:T(2,128)S(1)} copy-done((s32[512,2]{0,1:T(2,128)S(1)}, s32[512,2]{0,1:T(2,128)}, u32[]{:S(2)}) %copy-start.7) | copy-done | bytes 4120
  6.6 46.7 %gather_and_sum.1 = (f32[1,512]{1,0:T(1,128)S(1)}, bf16[448,512]{1,0:T(8,128)(2,1)S(1)}, bf16[512,1024]{1,0:T(8,128)(2,1)S(1)}) custom-call(bf16[384,3584]{1,0:T(8,128)(2,1)} %tokens.1, bf16[384,1024]{1,0:T(8,128)(2,1)S(1)} %copy-done.3, bf16[448,1024]{1,0:T(8,128)(2,1)S(1)} %copy-done.2, bf16[448,512]{1,0:T(8,128)(2,1)S(1)} %copy-done.4, ...), custom_call_target="tpu_custom_call" | custom-call | tf_op jit(solution)/shard_map/gather_and_sum/pallas_call | solution.py:347
  53.3 0.0 copy-start.1
  53.3 1.0 %copy-done.1 = bf16[512,1024]{1,0:T(8,128)(2,1)} copy-done((bf16[512,1024]{1,0:T(8,128)(2,1)}, bf16[512,1024]{1,0:T(8,128)(2,1)S(1)}, u32[]{:S(2)}) %copy-start.1) | copy-done | bytes 1048600
  54.2 0.0 copy-start.5
  54.2 0.8 %copy-done.5 = bf16[448,512]{1,0:T(8,128)(2,1)} copy-done((bf16[448,512]{1,0:T(8,128)(2,1)}, bf16[448,512]{1,0:T(8,128)(2,1)S(1)}, u32[]{:S(2)}) %copy-start.5) | copy-done | bytes 458776
  55.0 0.0 copy-start.8
  55.0 0.6 copy-done.8
  55.6 4.7 %finish.1 = (f32[448,1024]{1,0:T(8,128)}, f32[1,512]{1,0:T(1,128)}) custom-call(f32[1,512]{1,0:T(1,128)} %copy-done.8, s32[1,512]{1,0:T(1,128)} %bitcast.3, bf16[448,512]{1,0:T(8,128)(2,1)} %copy-done.5, bf16[512,1024]{1,0:T(8,128)(2,1)} %copy-done.1), custom_call_target="tpu_custom_call" | custom-call | tf_op jit(solution)/shard_map/finish/pallas_call | solution.py:411
Async XLA Ops:
  0.6 1.2 %copy-start = (bf16[512,1024]{1,0:T(8,128)(2,1)S(1)}, bf16[512,1024]{1,0:T(8,128)(2,1)}, u32[]{:S(2)}) copy-start(bf16[512,1024]{1,0:T(8,128)(2,1)} %factor_b.1) | copy-start | bytes 3145732
  1.9 1.2 %copy-start.2 = (bf16[448,1024]{1,0:T(8,128)(2,1)S(1)}, bf16[448,1024]{1,0:T(8,128)(2,1)}, u32[]{:S(2)}) copy-start(bf16[448,1024]{1,0:T(8,128)(2,1)} %weight.1) | copy-start | bytes 2752516
  3.0 1.1 %copy-start.3 = (bf16[384,1024]{1,0:T(8,128)(2,1)S(1)}, bf16[384,1024]{1,0:T(8,128)(2,1)}, u32[]{:S(2)}) copy-start(bf16[384,1024]{1,0:T(8,128)(2,1)} %target.1) | copy-start | bytes 2359300
  4.2 1.0 %copy-start.4 = (bf16[448,512]{1,0:T(8,128)(2,1)S(1)}, bf16[448,512]{1,0:T(8,128)(2,1)}, u32[]{:S(2)}) copy-start(bf16[448,512]{1,0:T(8,128)(2,1)} %factor_a.1) | copy-start | bytes 1376260
  5.2 0.7 %copy-start.6 = (s32[512]{0:T(512)S(1)}, s32[512]{0:T(512)}, u32[]{:S(2)}) copy-start(s32[512]{0:T(512)} %param.12) | copy-start | bytes 6148
  5.9 0.7 %copy-start.7 = (s32[512,2]{0,1:T(2,128)S(1)}, s32[512,2]{0,1:T(2,128)}, u32[]{:S(2)}) copy-start(s32[512,2]{0,1:T(2,128)} %param.13) | copy-start | bytes 12292
  53.3 1.0 %copy-start.1 = (bf16[512,1024]{1,0:T(8,128)(2,1)}, bf16[512,1024]{1,0:T(8,128)(2,1)S(1)}, u32[]{:S(2)}) copy-start(bf16[512,1024]{1,0:T(8,128)(2,1)S(1)} %get-tuple-element.9.bsel) | copy-start | bytes 3145732
  54.2 0.8 %copy-start.5 = (bf16[448,512]{1,0:T(8,128)(2,1)}, bf16[448,512]{1,0:T(8,128)(2,1)S(1)}, u32[]{:S(2)}) copy-start(bf16[448,512]{1,0:T(8,128)(2,1)S(1)} %get-tuple-element.8.asel) | copy-start | bytes 1376260
  55.0 0.6 copy-start.8

commit v2 on v1

--- a/solution.py
+++ b/solution.py
@@ -75,9 +75,9 @@
 
 
 def kernel(
-    tokens, target, weight, factor_a, factor_b, counts, index, totals, asel_out, bsel_out,
-    tok, tgt, buf, fb, fa, cnt, idx, acc_a, acc_w, owns, picks, brow, s_part, s_recv, asel, bsel,
-    ar_x, ar_y, ar_z, local, send_sem, recv_sem, tok_send, tok_recv, s_send, s_got, ar_send, ar_recv,
+    tokens, target, weight, factor_a, factor_b, counts, index, totals, asel, bsel,
+    tok, tgt, buf, fb, fa, cnt, idx, acc_a, acc_w, owns, picks, brow, s_part, s_recv,
+    ar_c, ar_xy, ar_z, local, send_sem, recv_sem, tok_send, tok_recv, s_send, s_got, ar_send, ar_recv,
 ):
     zh, x, c, zl, y = (lax.axis_index(n) for n in GRP_FSDP)
     z = zh * 2 + zl
@@ -97,6 +97,16 @@
 
     def columns(start, size):
         return pl.ds(pl.multiple_of(start, 128), size)
+
+    ar_peers = [
+        [dict(dc=1)],
+        [dict(dx=dx, dy=dy) for dx in range(4) for dy in range(4) if dx or dy],
+        [dict(dz=dz) for dz in range(1, 8)],
+    ]
+    barrier = pltpu.get_barrier_semaphore()
+    near = [dict(dc=1)] + [dict(dx=i) for i in (1, 3)] + [dict(dy=i) for i in (1, 3)] + [dict(dz=i) for i in (1, 7)]
+    for peer in near:
+        pl.semaphore_signal(barrier, inc=1, device_id=at(**peer), device_id_type=MESH)
 
     copies = {}
 
@@ -118,23 +128,7 @@
     bring("fb", factor_b, fb)
     bring("fa", factor_a, fa)
 
-    zero = jnp.zeros((64, 128), BF16)
-    for d in range(4):
-        gap = pl.multiple_of((1 - lax.rem(y + d, 2)) * depth, 64)
-        for o in range(2):
-            for j in range(6):
-                buf[o * 4 + d, j, pl.ds(gap, 64), :] = zero
-
-    ar_peers = [
-        [dict(dx=dx, dc=dc) for dx in range(4) for dc in range(2) if dx or dc],
-        [dict(dy=dy) for dy in range(1, 4)],
-        [dict(dz=dz) for dz in range(1, 8)],
-    ]
-    barrier = pltpu.get_barrier_semaphore()
-    for group in ar_peers:
-        for peer in group:
-            pl.semaphore_signal(barrier, inc=1, device_id=at(**peer), device_id_type=MESH)
-    pl.semaphore_wait(barrier, sum(map(len, ar_peers)))
+    pl.semaphore_wait(barrier, len(near))
 
     items = [item for link in INBOUND for item in INBOUND[link]]
     sends, waited = [], set()
@@ -182,6 +176,14 @@
     def start_swaps():
         for copy in swaps:
             copy.start()
+
+    def clear():
+        zero = jnp.zeros((64, 128), BF16)
+        for d in range(4):
+            gap = pl.multiple_of((1 - lax.rem(y + d, 2)) * depth, 64)
+            for o in range(2):
+                for j in range(6):
+                    buf[o * 4 + d, j, pl.ds(gap, 64), :] = zero
 
     def owners():
         copies["cnt"].wait()
@@ -216,15 +218,10 @@
             chosen = across(owns[i], right).astype(BF16)
             brow[i] = jnp.dot(chosen, mine, preferred_element_type=F32)
 
-    out_copies = []
-
     def chosen_left():
         copies["fa"].wait()
         left = one_hot(idx[0:1, :], 0, fa.shape[1])
         asel[...] = jnp.dot(fa[...], left, preferred_element_type=F32).astype(BF16)
-        copy = pltpu.make_async_copy(asel, asel_out, local.at[len(copies)])
-        copy.start()
-        out_copies.append(copy)
 
     def chosen_right():
         size = (cands, cands)
@@ -233,9 +230,6 @@
         column = jnp.sum(jnp.where(line == lane, row, 0.0), axis=1, keepdims=True)
         right = (column == lane.astype(F32)).astype(F32).astype(BF16)
         bsel[...] = jnp.dot(right, fb[...], preferred_element_type=F32).astype(BF16)
-        copy = pltpu.make_async_copy(bsel, bsel_out, local.at[len(copies) + 1])
-        copy.start()
-        out_copies.append(copy)
 
     seen, left_over = set(), {"a": 8}
     s_copies = [
@@ -287,7 +281,7 @@
     events = timeline()
     after_a = max(when for when, _, what in events if what[0] == "product" and what[2] == "a")
     events += [
-        (0.05, 2, (start_swaps,)), (0.5, 2, (owners,)), (1.0, 2, (left_picks,)), (1.5, 2, (right_rows,)),
+        (0.05, 2, (start_swaps,)), (0.1, 2, (clear,)), (0.5, 2, (owners,)), (1.0, 2, (left_picks,)), (1.5, 2, (right_rows,)),
         (2.0, 2, (chosen_left,)), (2.5, 2, (chosen_right,)), (after_a + 1.2, 2, (perturb,)),
     ]
     for _, _, what in sorted(events, key=lambda event: event[:2]):
@@ -307,8 +301,8 @@
         total += jnp.sum(owns[i].astype(F32) * loss, axis=0, keepdims=True)
     first = 0
     for group, ring, me, number in (
-        (ar_peers[0], ar_x, x * 2 + c, lambda dx=0, dc=0: lax.rem(x - dx + 4, 4) * 2 + lax.rem(c - dc + 2, 2)),
-        (ar_peers[1], ar_y, y, lambda dy: lax.rem(y - dy + 4, 4)),
+        (ar_peers[0], ar_c, c, lambda dc: 1 - c),
+        (ar_peers[1], ar_xy, x * 4 + y, lambda dx, dy: lax.rem(x - dx + 4, 4) * 4 + lax.rem(y - dy + 4, 4)),
         (ar_peers[2], ar_z, z, lambda dz: lax.rem(z - dz + 8, 8)),
     ):
         ring[me] = total
@@ -335,8 +329,6 @@
     totals[...] = total
     for copy in sends + swaps + s_copies:
         copy.wait_send()
-    for copy in out_copies:
-        copy.wait()
 
 
 def gather_and_sum(tokens, target, weight, factor_a, factor_b, counts, index):
@@ -352,12 +344,8 @@
             jax.ShapeDtypeStruct((depth, cands), BF16),
             jax.ShapeDtypeStruct((cands, out), BF16),
         ),
-        in_specs=[pl.BlockSpec(memory_space=pl.ANY)] * 7,
-        out_specs=(
-            pl.BlockSpec(memory_space=pltpu.VMEM),
-            pl.BlockSpec(memory_space=pl.ANY),
-            pl.BlockSpec(memory_space=pl.ANY),
-        ),
+        in_specs=[pl.BlockSpec(memory_space=pltpu.HBM)] * 7,
+        out_specs=(pl.BlockSpec(memory_space=pltpu.VMEM),) * 3,
         scratch_shapes=[
             pltpu.VMEM((2, rows, D), BF16),
             pltpu.VMEM((2, rows, out // 2), BF16),
@@ -373,53 +361,56 @@
             pltpu.VMEM((2, rows, out // 2), F32),
             pltpu.VMEM((2, rows, 128), F32),
             pltpu.VMEM((2, rows, 128), F32),
-            pltpu.VMEM((depth, cands), BF16),
-            pltpu.VMEM((cands, out), BF16),
+            pltpu.VMEM((2, 1, cands), F32),
+            pltpu.VMEM((16, 1, cands), F32),
             pltpu.VMEM((8, 1, cands), F32),
-            pltpu.VMEM((4, 1, cands), F32),
-            pltpu.VMEM((8, 1, cands), F32),
-            dma((14,)),
+            dma((12,)),
             dma((links,)),
             dma((links,)),
             dma((2,)),
             dma((2,)),
             dma((2,)),
             dma((2,)),
-            dma((17,)),
-            dma((17,)),
+            dma((23,)),
+            dma((23,)),
         ],
-        compiler_params=pltpu.CompilerParams(collective_id=0, has_side_effects=True, vmem_limit_bytes=48 << 20),
-    )(tokens, target, weight, factor_a, factor_b, counts, index)
-
-
-def finish_kernel(totals, counts, asel, bsel, update, scores):
-    cands = counts.shape[1]
+        compiler_params=pltpu.CompilerParams(collective_id=0, has_side_effects=True, vmem_limit_bytes=40 << 20),
+    )(*(pltpu.with_memory_space_constraint(a, pltpu.HBM) for a in (tokens, target, weight, factor_a, factor_b, counts, index)))
+
+
+def finish_kernel(totals, counts, asel, bsel, update, scores, block, sem):
+    cands, steps = counts.shape[1], block.shape[0]
+    size = block.shape[1]
     fitness = -totals[...] / counts[...].astype(F32)
     middle = jnp.mean(fitness, axis=1, keepdims=True)
     spread = jnp.mean((fitness - middle) ** 2, axis=1, keepdims=True)
     score = (fitness - middle) / jnp.sqrt(spread + 1e-06)
     scores[...] = score
-    scaled = (asel[...].astype(F32) * score).astype(BF16)
-    update[...] = jnp.dot(scaled, bsel[...], preferred_element_type=F32) * (cands**-0.5)
+    out = []
+    for k in range(steps):
+        lines = slice(k * size, (k + 1) * size)
+        scaled = (asel[lines, :].astype(F32) * score).astype(BF16)
+        block[k] = jnp.dot(scaled, bsel[...], preferred_element_type=F32) * (cands**-0.5)
+        copy = pltpu.make_async_copy(block.at[k], update.at[lines, :], sem.at[k])
+        copy.start()
+        out.append(copy)
+    for copy in out:
+        copy.wait()
 
 
 def finish(totals, counts, asel, bsel):
     depth, cands = asel.shape
     out = bsel.shape[1]
-    block = depth // 4
-    row = pl.BlockSpec((1, cands), lambda i: (0, 0))
+    steps = 4
+    vmem = pl.BlockSpec(memory_space=pltpu.VMEM)
     return pl.pallas_call(
         finish_kernel,
         name="finish",
-        grid=(4,),
         out_shape=(jax.ShapeDtypeStruct((depth, out), F32), jax.ShapeDtypeStruct((1, cands), F32)),
-        in_specs=[
-            row,
-            row,
-            pl.BlockSpec((block, cands), lambda i: (i, 0)),
-            pl.BlockSpec((cands, out), lambda i: (0, 0)),
-        ],
-        out_specs=(pl.BlockSpec((block, out), lambda i: (i, 0)), row),
+        in_specs=[vmem] * 4,
+        out_specs=(pl.BlockSpec(memory_space=pltpu.HBM), vmem),
+        scratch_shapes=[pltpu.VMEM((steps, depth // steps, out), F32), pltpu.SemaphoreType.DMA((steps,))],
+        compiler_params=pltpu.CompilerParams(vmem_limit_bytes=16 << 20),
     )(totals, counts, asel, bsel)
 
 

time: 60.7 us -> 47.6 us (0.78)
  local copies, waits for them, and re-layouts: 8.24 us -> 0.01 us
  Pallas kernels: 51.4 us -> 46.8 us
    unnamed x18 -> x2, local copies, waits for them, and re-layouts: 8.24 us -> 0.01 us
    pallas_call x1, Pallas kernels: 4.7 us -> 2.32 us  [finish(): pl.pallas_call(finish_kernel, name='finish', out_shape=(jax.ShapeDtypeStr...]
    pallas_call x1, Pallas kernels: 46.7 us -> 44.5 us  [gather_and_sum(): pl.pallas_call(kernel, name='gather_and_sum', out_shape=(jax.ShapeDtypeSt...]
where the time goes in v2:
time: 47.6 us; the launch traced here: 47.4 us
  Pallas kernels  46.8 us (98%)
  between operations  0.66 us (1%)
    pallas_call x1, Pallas kernels, gather_and_sum(): pl.pallas_call(kernel, name='gather_and_sum', out_shape=(jax.ShapeDtypeSt...  44.5 us
    pallas_call x1, Pallas kernels, finish(): pl.pallas_call(finish_kernel, name='finish', out_shape=(jax.ShapeDtypeStr...  2.32 us

profile of v2, /device:TPU:2, one launch (start us, length us, event | category | flops | bytes accessed | tf_op | source)
XLA Modules:
  0.0 47.4 jit_solution(5686724554582276183)
XLA Ops:
  0.6 0.0 copy-start
  0.6 44.5 %gather_and_sum.1 = (f32[1,512]{1,0:T(1,128)S(1)}, bf16[448,512]{1,0:T(8,128)(2,1)S(1)}, bf16[512,1024]{1,0:T(8,128)(2,1)S(1)}) custom-call(bf16[384,3584]{1,0:T(8,128)(2,1)} %tokens.1, bf16[384,1024]{1,0:T(8,128)(2,1)} %target.1, bf16[448,1024]{1,0:T(8,128)(2,1)} %weight.1, bf16[448,512]{1,0:T(8,128)(2,1)} %factor_a.1, bf16[512,1024]{1,0:T(8,128)(2,1)} %factor_b.1, ...), custom_call_target="tpu_custom_call" | custom-call | tf_op jit(solution)/shard_map/gather_and_sum/pallas_call | solution.py:339
  45.1 0.0 copy-done
  45.1 2.3 %finish.1 = (f32[448,1024]{1,0:T(8,128)}, f32[1,512]{1,0:T(1,128)}) custom-call(f32[1,512]{1,0:T(1,128)S(1)} %get-tuple-element.7.totals, s32[1,512]{1,0:T(1,128)S(1)} %bitcast.4, bf16[448,512]{1,0:T(8,128)(2,1)S(1)} %get-tuple-element.8.asel, bf16[512,1024]{1,0:T(8,128)(2,1)S(1)} %get-tuple-element.9.bsel), custom_call_target="tpu_custom_call" | custom-call | tf_op jit(solution)/shard_map/finish/pallas_call | solution.py:406
Async XLA Ops:
  0.6 44.5 %copy-start = (s32[512]{0:T(512)S(1)}, s32[512]{0:T(512)}, u32[]{:S(2)}) copy-start(s32[512]{0:T(512)} %param.12) | copy-start | bytes 6148

commit v3 on v2

--- a/solution.py
+++ b/solution.py
@@ -16,32 +16,55 @@
 GRP_FSDP = ("grp_0", "grp_1", "grp_2", "fsdp_0", "fsdp_1")
 
 INBOUND = {
-    "y+": ((0, 1, "m1"), (0, 1, "m2"), (0, 2, "m1"), (0, 1, "c2"), (0, 1, "c1"), (0, 2, "m2"), (0, 2, "c1"), (1, 2, "t2")),
-    "y-": ((0, 3, "m1"), (0, 3, "m2"), (0, 3, "c1"), (0, 3, "c2"), (1, 3, "m2"), (0, 2, "c2"), (1, 2, "m2"), (1, 2, "c1")),
-    "z+": ((1, 0, "m1"), (1, 0, "t1"), (1, 3, "m1"), (1, 1, "m1"), (1, 1, "t1"), (1, 3, "c1"), (1, 1, "c2"), (1, 2, "c2")),
-    "z-": ((1, 0, "m2"), (1, 0, "c1"), (1, 0, "c2"), (1, 1, "m2"), (1, 2, "m1"), (1, 3, "c2"), (1, 1, "c1")),
-    "x+": ((0, 1, "t1"), (1, 0, "t2"), (1, 3, "t1"), (0, 3, "t2"), (1, 3, "t2"), (0, 2, "t2")),
-    "x-": ((0, 3, "t1"), (0, 1, "t2"), (0, 2, "t1"), (1, 1, "t2"), (1, 2, "t1")),
+    "y+": (
+        (0, 1, "m1", 0), (0, 1, "m1", 1), (0, 1, "m2", 0), (0, 1, "m2", 1), (0, 2, "m1", 1), (0, 2, "m1", 0),
+        (0, 2, "m2", 0), (0, 1, "c2", 1), (0, 1, "c1", 1), (0, 1, "c1", 0), (0, 1, "c2", 0), (1, 1, "c1", 1),
+        (1, 1, "c2", 1), (0, 2, "c2", 1), (1, 2, "c1", 1),
+    ),
+    "y-": (
+        (0, 3, "m1", 0), (0, 3, "m1", 1), (0, 3, "m2", 1), (0, 3, "m2", 0), (1, 3, "m1", 1), (0, 2, "m2", 1),
+        (0, 3, "c2", 1), (0, 3, "c2", 0), (0, 3, "c1", 0), (0, 3, "c1", 1), (0, 2, "c2", 0), (0, 2, "c1", 0),
+        (1, 3, "c1", 1), (0, 2, "c1", 1), (1, 2, "c2", 1),
+    ),
+    "z+": (
+        (1, 0, "m1", 0), (1, 0, "m2", 0), (1, 0, "t1", 0), (1, 1, "m1", 0), (1, 1, "m1", 1), (1, 0, "c2", 0),
+        (1, 0, "c1", 0), (1, 1, "m2", 0), (1, 3, "m2", 0), (1, 2, "m1", 0), (1, 2, "m2", 0), (1, 2, "m2", 1),
+        (1, 3, "c2", 0), (1, 1, "c2", 0), (1, 2, "c2", 0),
+    ),
+    "z-": (
+        (1, 0, "m1", 1), (1, 0, "m2", 1), (1, 0, "t1", 1), (1, 3, "m1", 0), (1, 0, "c1", 1), (1, 0, "c2", 1),
+        (1, 1, "m2", 1), (1, 3, "m2", 1), (1, 0, "t2", 0), (1, 2, "m1", 1), (1, 3, "c2", 1), (1, 3, "c1", 0),
+        (1, 2, "t1", 0), (1, 1, "c1", 0), (1, 2, "c1", 0),
+    ),
+    "x+": (
+        (0, 3, "t1", 0), (0, 1, "t1", 1), (0, 1, "t2", 0), (0, 3, "t2", 1), (1, 1, "t1", 1), (0, 1, "t2", 1),
+        (1, 1, "t1", 0), (0, 2, "t1", 0), (1, 1, "t2", 0), (0, 2, "t2", 1), (0, 2, "t2", 0), (1, 2, "t2", 0),
+    ),
+    "x-": (
+        (0, 1, "t1", 0), (0, 3, "t1", 1), (1, 0, "t2", 1), (0, 3, "t2", 0), (1, 3, "t1", 0), (0, 2, "t1", 1),
+        (1, 3, "t1", 1), (1, 3, "t2", 1), (1, 1, "t2", 1), (1, 3, "t2", 0), (1, 2, "t1", 1), (1, 2, "t2", 1),
+    ),
 }
 LINK_STEP = {"y+": (0, 1, 0), "y-": (0, -1, 0), "z+": (0, 0, 1), "z-": (0, 0, -1), "x+": (1, 0, 0), "x-": (-1, 0, 0)}
 SWAP = {"m1": "t1", "m2": "t2", "t1": "m1", "t2": "m2"}
 ROLES = ("m1", "m2", "t1", "t2", "c1", "c2")
 GROUPS = {"a": ("m1", "t1"), "p": ("m2", "t2"), "q": ("c1", "c2")}
-PIECE_US, HOP_US, LEAD_US, TOKENS_US = 2.48, 1.7, 2.5, 5.0
-
-
-def source(link, o, d, role):
+PARTS = 2
+PIECE_US, HOP_US, LEAD_US, TOKENS_US, LATE_US = 2.48 / PARTS, 1.7, 1.25, 5.0, 1.5
+
+
+def source(link, o, d, role, part):
     if link == "y+":
-        return (o, (d - 1) % 4, role)
+        return (o, (d - 1) % 4, role, part)
     if link == "y-":
-        return (o, (d + 1) % 4, role)
+        return (o, (d + 1) % 4, role, part)
     if link[0] == "z":
-        return (1 - o, d, role)
-    return (o, d, SWAP[role])
+        return (1 - o, d, role, part)
+    return (o, d, SWAP[role], part)
 
 
 def timeline():
-    arrival = {(0, 0, role): 0.0 for role in ROLES}
+    arrival = {(0, 0, role, part): 0.0 for role in ROLES for part in range(PARTS)}
     free = dict.fromkeys(INBOUND, 0.0)
     waiting = {link: list(items) for link, items in INBOUND.items()}
     events = []
@@ -60,8 +83,8 @@
     for o in range(2):
         for d in range(4):
             for group, roles in GROUPS.items():
-                when = max(TOKENS_US, *(arrival[(o, d, role)] for role in roles))
-                events.append((when, 1, ("product", (o, d), group)))
+                when = max(TOKENS_US, *(arrival[(o, d, role, part)] for role in roles for part in range(PARTS)))
+                events.append((when + LATE_US, 1, ("product", (o, d), group)))
     return events
 
 
@@ -92,8 +115,9 @@
     def piece_of(role):
         return {"m1": par, "m2": 2 + par, "t1": 1 - par, "t2": 3 - par, "c1": 4, "c2": 5}[role]
 
-    def rows_of(d):
-        return pl.ds(pl.multiple_of(lax.rem(y + d, 2) * 64, 64), depth)
+    def rows_of(d, part=0, parts=1):
+        size = depth // parts
+        return pl.ds(pl.multiple_of(lax.rem(y + d, 2) * 64 + part * size, 32), size)
 
     def columns(start, size):
         return pl.ds(pl.multiple_of(start, 128), size)
@@ -137,26 +161,27 @@
         if item in waited:
             return
         waited.add(item)
-        o, d, role = item
+        o, d, role, part = item
         if (o, d) == (0, 0):
-            copies[role].wait()
+            if part == 0:
+                copies[role].wait()
             return
         k = items.index(item)
-        place = buf.at[o * 4 + d, piece_of(role), rows_of(d)]
+        place = buf.at[o * 4 + d, piece_of(role), rows_of(d, part, PARTS)]
         pltpu.make_async_remote_copy(
             src_ref=place, dst_ref=place, send_sem=send_sem.at[k], recv_sem=recv_sem.at[k],
             device_id=at(dc=1), device_id_type=MESH,
         ).wait_recv()
 
     def send(link, item):
-        so, sd, srole = source(link, *item)
-        need((so, sd, srole))
+        so, sd, srole, part = source(link, *item)
+        need((so, sd, srole, 0 if (so, sd) == (0, 0) else part))
         k = items.index(item)
         dx, dy, dz = LINK_STEP[link]
         j = piece_of(srole)
         copy = pltpu.make_async_remote_copy(
-            src_ref=buf.at[so * 4 + sd, j, rows_of(sd)],
-            dst_ref=buf.at[item[0] * 4 + item[1], j, rows_of(sd)],
+            src_ref=buf.at[so * 4 + sd, j, rows_of(sd, part, PARTS)],
+            dst_ref=buf.at[item[0] * 4 + item[1], j, rows_of(sd, part, PARTS)],
             send_sem=send_sem.at[k], recv_sem=recv_sem.at[k],
             device_id=at(-dx, -dy, -dz), device_id_type=MESH,
         )
@@ -243,7 +268,8 @@
     def product(slot, group):
         o, d = slot
         for role in GROUPS[group]:
-            need((o, d, role))
+            for part in range(PARTS):
+                need((o, d, role, part))
         first = lax.rem(zl + o, 2) * 4 + lax.rem(y + d, 4)
         window = columns(first // 2 * 896 + lax.rem(first, 2) * 384, 512)
         j = "apq".index(group) * 2
@@ -282,7 +308,7 @@
     after_a = max(when for when, _, what in events if what[0] == "product" and what[2] == "a")
     events += [
         (0.05, 2, (start_swaps,)), (0.1, 2, (clear,)), (0.5, 2, (owners,)), (1.0, 2, (left_picks,)), (1.5, 2, (right_rows,)),
-        (2.0, 2, (chosen_left,)), (2.5, 2, (chosen_right,)), (after_a + 1.2, 2, (perturb,)),
+        (after_a + 1.2, 2, (perturb,)),
     ]
     for _, _, what in sorted(events, key=lambda event: event[:2]):
         if what[0] == "send":
@@ -315,6 +341,9 @@
         ]
         for copy in out:
             copy.start()
+        if group is ar_peers[1]:
+            chosen_left()
+            chosen_right()
         for k, peer in enumerate(group):
             place = ring.at[number(**peer)]
             pltpu.make_async_remote_copy(

time: 47.6 us -> 46.4 us (0.975)
  Pallas kernels: 46.8 us -> 45.6 us
    pallas_call x1, Pallas kernels: 44.5 us -> 43.3 us  [gather_and_sum(): pl.pallas_call(kernel, name='gather_and_sum', out_shape=(jax.ShapeDtypeSt...]
where the time goes in v3:
time: 46.4 us; the launch traced here: 46.3 us
  Pallas kernels  45.6 us (98%)
  between operations  0.66 us (1%)
    pallas_call x1, Pallas kernels, gather_and_sum(): pl.pallas_call(kernel, name='gather_and_sum', out_shape=(jax.ShapeDtypeSt...  43.3 us
    pallas_call x1, Pallas kernels, finish(): pl.pallas_call(finish_kernel, name='finish', out_shape=(jax.ShapeDtypeStr...  2.31 us

profile of v3, /device:TPU:2, one launch (start us, length us, event | category | flops | bytes accessed | tf_op | source)
XLA Modules:
  0.0 46.3 jit_solution(10062381377528105007)
XLA Ops:
  0.6 0.0 copy-start
  0.6 43.3 %gather_and_sum.1 = (f32[1,512]{1,0:T(1,128)S(1)}, bf16[448,512]{1,0:T(8,128)(2,1)S(1)}, bf16[512,1024]{1,0:T(8,128)(2,1)S(1)}) custom-call(bf16[384,3584]{1,0:T(8,128)(2,1)} %tokens.1, bf16[384,1024]{1,0:T(8,128)(2,1)} %target.1, bf16[448,1024]{1,0:T(8,128)(2,1)} %weight.1, bf16[448,512]{1,0:T(8,128)(2,1)} %factor_a.1, bf16[512,1024]{1,0:T(8,128)(2,1)} %factor_b.1, ...), custom_call_target="tpu_custom_call" | custom-call | tf_op jit(solution)/shard_map/gather_and_sum/pallas_call | solution.py:368
  44.0 0.0 copy-done
  44.0 2.3 %finish.1 = (f32[448,1024]{1,0:T(8,128)}, f32[1,512]{1,0:T(1,128)}) custom-call(f32[1,512]{1,0:T(1,128)S(1)} %get-tuple-element.7.totals, s32[1,512]{1,0:T(1,128)S(1)} %bitcast.4, bf16[448,512]{1,0:T(8,128)(2,1)S(1)} %get-tuple-element.8.asel, bf16[512,1024]{1,0:T(8,128)(2,1)S(1)} %get-tuple-element.9.bsel), custom_call_target="tpu_custom_call" | custom-call | tf_op jit(solution)/shard_map/finish/pallas_call | solution.py:435
Async XLA Ops:
  0.6 43.4 %copy-start = (s32[512]{0:T(512)S(1)}, s32[512]{0:T(512)}, u32[]{:S(2)}) copy-start(s32[512]{0:T(512)} %param.12) | copy-start | bytes 6148

commit v4 on v3

--- a/solution.py
+++ b/solution.py
@@ -124,8 +124,8 @@
 
     ar_peers = [
         [dict(dc=1)],
-        [dict(dx=dx, dy=dy) for dx in range(4) for dy in range(4) if dx or dy],
-        [dict(dz=dz) for dz in range(1, 8)],
+        [dict(dx=dx, dy=dy) for dx in (2, 1, 3, 0) for dy in (2, 1, 3, 0) if dx or dy],
+        [dict(dz=dz) for dz in (4, 3, 5, 2, 6, 1, 7)],
     ]
     barrier = pltpu.get_barrier_semaphore()
     near = [dict(dc=1)] + [dict(dx=i) for i in (1, 3)] + [dict(dy=i) for i in (1, 3)] + [dict(dz=i) for i in (1, 7)]

time: 46.4 us -> 46.3 us (level)
  no operation moved by 1% of the time
where the time goes in v4:
time: 46.3 us; the launch traced here: 46.2 us
  Pallas kernels  45.6 us (98%)
  between operations  0.66 us (1%)
    pallas_call x1, Pallas kernels, gather_and_sum(): pl.pallas_call(kernel, name='gather_and_sum', out_shape=(jax.ShapeDtypeSt...  43.2 us
    pallas_call x1, Pallas kernels, finish(): pl.pallas_call(finish_kernel, name='finish', out_shape=(jax.ShapeDtypeStr...  2.32 us

profile of v4, /device:TPU:2, one launch (start us, length us, event | category | flops | bytes accessed | tf_op | source)
XLA Modules:
  0.0 46.2 jit_solution(1032899845455954367)
XLA Ops:
  0.6 0.0 copy-start
  0.6 43.2 %gather_and_sum.1 = (f32[1,512]{1,0:T(1,128)S(1)}, bf16[448,512]{1,0:T(8,128)(2,1)S(1)}, bf16[512,1024]{1,0:T(8,128)(2,1)S(1)}) custom-call(bf16[384,3584]{1,0:T(8,128)(2,1)} %tokens.1, bf16[384,1024]{1,0:T(8,128)(2,1)} %target.1, bf16[448,1024]{1,0:T(8,128)(2,1)} %weight.1, bf16[448,512]{1,0:T(8,128)(2,1)} %factor_a.1, bf16[512,1024]{1,0:T(8,128)(2,1)} %factor_b.1, ...), custom_call_target="tpu_custom_call" | custom-call | tf_op jit(solution)/shard_map/gather_and_sum/pallas_call | solution.py:368
  43.9 0.0 copy-done
  43.9 2.3 %finish.1 = (f32[448,1024]{1,0:T(8,128)}, f32[1,512]{1,0:T(1,128)}) custom-call(f32[1,512]{1,0:T(1,128)S(1)} %get-tuple-element.7.totals, s32[1,512]{1,0:T(1,128)S(1)} %bitcast.4, bf16[448,512]{1,0:T(8,128)(2,1)S(1)} %get-tuple-element.8.asel, bf16[512,1024]{1,0:T(8,128)(2,1)S(1)} %get-tuple-element.9.bsel), custom_call_target="tpu_custom_call" | custom-call | tf_op jit(solution)/shard_map/finish/pallas_call | solution.py:435
Async XLA Ops:
  0.6 43.3 %copy-start = (s32[512]{0:T(512)S(1)}, s32[512]{0:T(512)}, u32[]{:S(2)}) copy-start(s32[512]{0:T(512)} %param.12) | copy-start | bytes 6148

commit v5 on v4

--- a/solution.py
+++ b/solution.py
@@ -430,7 +430,7 @@
 def finish(totals, counts, asel, bsel):
     depth, cands = asel.shape
     out = bsel.shape[1]
-    steps = 4
+    steps = 7
     vmem = pl.BlockSpec(memory_space=pltpu.VMEM)
     return pl.pallas_call(
         finish_kernel,

time: 46.3 us -> 46.9 us (1.013)
  Pallas kernels: 45.6 us -> 46.1 us
    pallas_call x1, Pallas kernels: 2.32 us -> 2.9 us  [finish(): pl.pallas_call(finish_kernel, name='finish', out_shape=(jax.ShapeDtypeStr...]
where the time goes in v5:
time: 46.9 us; the launch traced here: 46.8 us
  Pallas kernels  46.1 us (98%)
  between operations  0.66 us (1%)
    pallas_call x1, Pallas kernels, gather_and_sum(): pl.pallas_call(kernel, name='gather_and_sum', out_shape=(jax.ShapeDtypeSt...  43.2 us
    pallas_call x1, Pallas kernels, finish(): pl.pallas_call(finish_kernel, name='finish', out_shape=(jax.ShapeDtypeStr...  2.9 us

profile of v5, /device:TPU:2, one launch (start us, length us, event | category | flops | bytes accessed | tf_op | source)
XLA Modules:
  0.0 46.8 jit_solution(15009697742711706871)
XLA Ops:
  0.6 0.0 copy-start
  0.6 43.2 %gather_and_sum.1 = (f32[1,512]{1,0:T(1,128)S(1)}, bf16[448,512]{1,0:T(8,128)(2,1)S(1)}, bf16[512,1024]{1,0:T(8,128)(2,1)S(1)}) custom-call(bf16[384,3584]{1,0:T(8,128)(2,1)} %tokens.1, bf16[384,1024]{1,0:T(8,128)(2,1)} %target.1, bf16[448,1024]{1,0:T(8,128)(2,1)} %weight.1, bf16[448,512]{1,0:T(8,128)(2,1)} %factor_a.1, bf16[512,1024]{1,0:T(8,128)(2,1)} %factor_b.1, ...), custom_call_target="tpu_custom_call" | custom-call | tf_op jit(solution)/shard_map/gather_and_sum/pallas_call | solution.py:368
  43.9 0.0 copy-done
  43.9 2.9 %finish.1 = (f32[448,1024]{1,0:T(8,128)}, f32[1,512]{1,0:T(1,128)}) custom-call(f32[1,512]{1,0:T(1,128)S(1)} %get-tuple-element.7.totals, s32[1,512]{1,0:T(1,128)S(1)} %bitcast.4, bf16[448,512]{1,0:T(8,128)(2,1)S(1)} %get-tuple-element.8.asel, bf16[512,1024]{1,0:T(8,128)(2,1)S(1)} %get-tuple-element.9.bsel), custom_call_target="tpu_custom_call" | custom-call | tf_op jit(solution)/shard_map/finish/pallas_call | solution.py:435
Async XLA Ops:
  0.6 43.3 %copy-start = (s32[512]{0:T(512)S(1)}, s32[512]{0:T(512)}, u32[]{:S(2)}) copy-start(s32[512]{0:T(512)} %param.12) | copy-start | bytes 6148
